TPU v7x, 256 devices: a whole 4x4x8 slice. The times are simulated.
256 devices in a mesh: ctx: 8 (over z_lo, core), dp: 8 (over z_hi, y), head: 4 (over x).
Axes of the slice: x: 4, y: 4, z: 8 (z_hi: 2, z_lo: 4; z = z_hi * 4 + z_lo), core: 2. Of those that a mesh axis runs over, the one named last changes fastest.
Arguments:
- queries: bfloat16 [32768, 8, 128], P(('dp', 'ctx'), 'head'), parts along dimension 0, may hold values from -40 to 40
- keys: bfloat16 [32768, 128], P(('dp', 'ctx')), parts along dimension 0, may hold values from -6 to 6
- values: bfloat16 [32768, 128], P(('dp', 'ctx')), parts along dimension 0, may hold values from -6 to 6
- output: bfloat16 [32768, 8, 128], P(('dp', 'ctx'), 'head'), parts along dimension 0, may hold values from -6 to 6
- output_grad: bfloat16 [32768, 8, 128], P(('dp', 'ctx'), 'head'), parts along dimension 0, may hold values from -6 to 6
- block_doc: int32 [256], P('dp'), parts along dimension 0, may hold values from 0 to 3, never falling along the last dimension, each value on 1 to 24 neighbouring positions
Outputs:
- query_grad: bfloat16 [32768, 8, 128], P(('dp', 'ctx'), 'head'), parts along dimension 0
- key_grad: bfloat16 [32768, 128], P(('dp', 'ctx', 'head')), parts along dimension 0
- value_grad: bfloat16 [32768, 128], P(('dp', 'ctx', 'head')), parts along dimension 0
There are 8 independent parts, one for each index of `dp`. A program takes and returns all parts, laid end to end along the dimension named above; each array names one. Nothing has to cross between parts.
Inputs may be any that keep to these rules, and one draw needn't show every extreme that they name: block_doc[b] is the document of tokens b * 128 to (b + 1) * 128 - 1; ids never fall; each of the 4 documents spans 1 to 24 blocks, and one spans exactly 24.
All inputs are finite; a program needn't handle non-finite values.
Results may differ from a plain program's by a relative error of at most 0.0049.
Values may be sent and summed in bfloat16 or wider, within the bound.
No kernel may reach another device: no remote copies, remote signals or barrier semaphores. Data moves between devices by JAX's collectives and lax.ppermute only.
A program may use at most 64 MiB of HBM per device.

v0:
```python
import jax
import jax.numpy as jnp
from jax import lax
from jax.sharding import PartitionSpec as P

BLK = 128
masked_score = -1e30


def local(queries, keys, values, output, output_grad, block_doc):
    shard_rows = queries.shape[0]
    heads_here = queries.shape[1]
    head_size = queries.shape[2]
    cycle_length = lax.axis_size("ctx")
    seq_tokens = shard_rows * cycle_length
    ctx_index = lax.axis_index("ctx")
    inv_root = head_size ** (-0.5)
    doc_tok = jnp.broadcast_to(block_doc[:, None], (block_doc.shape[0], BLK)).reshape(seq_tokens)
    row_ids = jnp.arange(shard_rows, dtype=jnp.int32)

    def positions_of(anchor):
        return anchor * shard_rows + row_ids

    query_pos = positions_of(ctx_index)
    query_doc = jnp.take(doc_tok, query_pos)
    row_delta = jnp.sum(output_grad.astype(jnp.float32) * output.astype(jnp.float32), axis=-1)

    def visible(anchor):
        key_pos = positions_of(anchor)
        key_doc = jnp.take(doc_tok, key_pos)
        return (key_pos[None, :] <= query_pos[:, None]) & (key_doc[None, :] == query_doc[:, None])

    def scores(key_tile, visible_mask):
        score_tile = (
            jnp.einsum("bhd,kd->bhk", queries, key_tile, preferred_element_type=jnp.float32)
            * inv_root
        )
        return jnp.where(visible_mask[:, None, :], score_tile, masked_score)

    def stat_step(stats_pair, key_tile, anchor):
        visible_mask = visible(anchor)
        running_max, running_sum = stats_pair
        score_tile = scores(key_tile, visible_mask)
        new_max = jnp.maximum(running_max, jnp.max(score_tile, axis=-1))
        terms = jnp.where(visible_mask[:, None, :], jnp.exp(score_tile - new_max[..., None]), 0.0)
        return (new_max, running_sum * jnp.exp(running_max - new_max) + jnp.sum(terms, axis=-1))

    def grad_step(key_tile, value_tile, anchor, log_total):
        visible_mask = visible(anchor)
        score_tile = scores(key_tile, visible_mask)
        prob = jnp.where(visible_mask[:, None, :], jnp.exp(score_tile - log_total[..., None]), 0.0)
        prob_low = prob.astype(jnp.bfloat16)
        prob_grad = jnp.einsum(
            "bhd,kd->bhk", output_grad, value_tile, preferred_element_type=jnp.float32
        )
        score_grad = (prob * (prob_grad - row_delta[..., None])).astype(jnp.bfloat16)
        query_part = (
            jnp.einsum("bhk,kd->bhd", score_grad, key_tile, preferred_element_type=jnp.float32)
            * inv_root
        )
        key_part = (
            jnp.einsum("bhk,bhd->kd", score_grad, queries, preferred_element_type=jnp.float32)
            * inv_root
        )
        value_part = jnp.einsum(
            "bhk,bhd->kd", prob_low, output_grad, preferred_element_type=jnp.float32
        )
        return (query_part, jnp.stack([key_part, value_part], axis=1))

    stats_start = (
        jnp.full((shard_rows, heads_here), masked_score, jnp.float32),
        jnp.zeros((shard_rows, heads_here), jnp.float32),
    )
    query_start = jnp.zeros((shard_rows, heads_here, head_size), jnp.float32)
    key_all, value_all = (
        lax.all_gather(keys, "ctx", axis=0, tiled=True),
        lax.all_gather(values, "ctx", axis=0, tiled=True),
    )

    def stat_loop(step_index, stats_pair):
        key_tile = lax.dynamic_slice_in_dim(key_all, step_index * shard_rows, shard_rows, 0)
        return stat_step(stats_pair, key_tile, step_index)

    running_max, running_sum = lax.fori_loop(0, cycle_length, stat_loop, stats_start)
    log_total = running_max + jnp.log(running_sum)

    def grad_loop(query_acc, step_index):
        key_tile = lax.dynamic_slice_in_dim(key_all, step_index * shard_rows, shard_rows, 0)
        value_tile = lax.dynamic_slice_in_dim(value_all, step_index * shard_rows, shard_rows, 0)
        query_part, pair_part = grad_step(key_tile, value_tile, step_index, log_total)
        return (query_acc + query_part, pair_part)

    query_acc, pair_blocks = lax.scan(
        grad_loop, query_start, jnp.arange(cycle_length, dtype=jnp.int32)
    )
    partial_grads = pair_blocks.reshape(seq_tokens, 2, head_size)
    owned_rows = lax.psum_scatter(partial_grads, ("ctx", "head"), scatter_dimension=0, tiled=True)
    query_grad = query_acc.astype(jnp.bfloat16)
    key_grad = owned_rows[:, 0, :].astype(jnp.bfloat16)
    value_grad = owned_rows[:, 1, :].astype(jnp.bfloat16)
    return (query_grad, key_grad, value_grad)


def solution(mesh):
    placed = (
        P(("dp", "ctx"), "head", None),
        P(("dp", "ctx"), None),
        P(("dp", "ctx"), None),
        P(("dp", "ctx"), "head", None),
        P(("dp", "ctx"), "head", None),
        P("dp"),
    )
    return jax.shard_map(
        local,
        mesh=mesh,
        in_specs=placed,
        out_specs=(
            P(("dp", "ctx"), "head", None),
            P(("dp", "ctx", "head"), None),
            P(("dp", "ctx", "head"), None),
        ),
        check_vma=False,
    )
```

profile of v0, /device:TPU:24, one launch (start us, length us, event | category | flops | bytes accessed | tf_op | source)
XLA Modules:
  0.0 344.0 jit_solution(15952463932650075983)
XLA Ops:
  8.8 0.7 broadcast_bitcast_fusion.2
  9.5 3.1 gather_fusion.2
  13.6 36.0 %all-gather.3.cloned.1.call-done = bf16[4096,128]{1,0:T(8,128)(2,1)} async-done(((bf16[512,128]{1,0:T(8,128)(2,1)}), bf16[4096,128]{1,0:T(8,128)(2,1)}) %all-gather.3.cloned.1.call-update) | async-done | bytes 1048592 | tf_op jit(solution)/shard_map/all_gather | solution.py:76
  49.6 45.2 %while.29 = (s32[]{:T(128)}, f32[512,2]{0,1:T(2,128)S(1)}, f32[512,2]{0,1:T(2,128)S(1)}, s32[512]{0:T(512)S(1)}, bf16[4096,128]{1,0:T(8,128)(2,1)}, /*index=5*/b...) while((s32[]{:T(128)}, f32[512,2]{0,1:T(2,128)S(1)}, ...), condition=%wide.region_3.5_spmd.clone, body=%wide.region_0.4_spmd.clone.sunk | while | flops 139211264 | bytes 5474630 | solution.py:84
  49.7 3.1 gather_fusion
  53.1 1.5 fusion.64
  55.4 3.1 gather_fusion
  58.8 1.5 fusion.64
  61.0 3.1 gather_fusion
  64.4 1.5 fusion.64
  66.7 3.1 gather_fusion
  70.1 1.5 fusion.64
  72.3 3.1 gather_fusion
  75.7 1.5 fusion.64
  78.0 3.1 gather_fusion
  81.4 1.5 fusion.64
  83.6 3.1 gather_fusion
  87.0 1.5 fusion.64
  89.3 3.1 gather_fusion
  92.7 1.5 fusion.64
  94.8 89.5 %while.30 = (s32[]{:T(128)}, f32[512,2,128]{2,0,1:T(8,128)S(1)}, f32[8,512,2,128]{3,1,0,2:T(8,128)}, s32[8]{0:T(128)S(1)}, s32[512]{0:T(512)S(1)}, /*index=5*/bf...) while((s32[]{:T(128)}, f32[512,2,128]{2,0,1:T(8,128)S(1)}, ...), condition=%wide.region_6.8_spmd.clone, body=%wide.region_5.7_spmd.clone.sunk | while | flops 676666880 | bytes 14080389 | solution.py:93
  96.2 3.1 gather_fusion.1
  99.7 1.7 fusion.77
  101.8 1.4 fusion.78
  103.6 1.6 fusion.79
  105.2 0.9 fusion.81
  107.4 3.1 gather_fusion.1
  110.9 1.7 fusion.77
  113.0 1.4 fusion.78
  114.8 1.6 fusion.79
  116.4 0.8 fusion.81
  118.6 3.1 gather_fusion.1
  122.0 1.7 fusion.77
  124.2 1.4 fusion.78
  126.0 1.6 fusion.79
  127.6 0.8 fusion.81
  129.8 3.1 gather_fusion.1
  133.2 1.7 fusion.77
  135.3 1.4 fusion.78
  137.2 1.6 fusion.79
  138.8 0.8 fusion.81
  141.0 3.1 gather_fusion.1
  144.4 1.7 fusion.77
  146.5 1.4 fusion.78
  148.4 1.6 fusion.79
  150.0 0.8 fusion.81
  152.1 3.1 gather_fusion.1
  155.6 1.7 fusion.77
  157.7 1.4 fusion.78
  159.5 1.6 fusion.79
  161.1 0.8 fusion.81
  163.3 3.1 gather_fusion.1
  166.8 1.7 fusion.77
  168.9 1.4 fusion.78
  170.7 1.6 fusion.79
  172.3 0.8 fusion.81
  174.5 3.1 gather_fusion.1
  177.9 1.7 fusion.77
  180.1 1.4 fusion.78
  181.9 1.6 fusion.79
  183.5 0.8 fusion.81
  184.4 1.1 copy.33
  185.5 150.5 %reduce-scatter.2.cloned.1.call-done = f32[128,2,128]{2,0,1:T(8,128)} async-done(((f32[4096,2,128]{2,0,1:T(8,128)}), f32[128,2,128]{2,0,1:T(8,128)}) %reduce-scatter.2.cloned.1.call-update) | async-done | bytes 131088 | tf_op jit(solution)/shard_map/reduce_scatter | solution.py:97
  335.9 0.9 convert.4
  (181 shorter events, 25.5 us)
Async XLA Ops:
  7.2 5.5 %copy-start.2 = (bf16[512,2,128]{2,1,0:T(2,128)(2,1)S(1)}, bf16[512,2,128]{2,1,0:T(2,128)(2,1)}, u32[]{:S(2)}) copy-start(bf16[512,2,128]{2,1,0:T(2,128)(2,1)} %param.12) | copy-start | bytes 786436
  7.2 5.6 %copy-start = (bf16[512,2,128]{2,1,0:T(2,128)(2,1)S(1)}, bf16[512,2,128]{2,1,0:T(2,128)(2,1)}, u32[]{:S(2)}) copy-start(bf16[512,2,128]{2,1,0:T(2,128)(2,1)} %param.16) | copy-start | bytes 786436
  7.2 5.6 %copy-start.1 = (bf16[512,2,128]{2,1,0:T(2,128)(2,1)S(1)}, bf16[512,2,128]{2,1,0:T(2,128)(2,1)}, u32[]{:S(2)}) copy-start(bf16[512,2,128]{2,1,0:T(2,128)(2,1)} %param.15) | copy-start | bytes 786436
  7.2 42.4 %all-gather.3.cloned.1.call-start = ((), (), s32[]{:S(2)}) async-start(), calls=%async_computation.1 | async-start | bytes 1179648 | tf_op jit(solution)/shard_map/all_gather | solution.py:76
  7.9 86.9 %all-gather.5.cloned.1.call-start = ((), (), s32[]{:S(2)}) async-start(), calls=%async_computation.2 | async-start | bytes 1179648 | tf_op jit(solution)/shard_map/all_gather | solution.py:77
  8.7 327.3 %reduce-scatter.2.cloned.1.call-start = ((), (), s32[]{:S(2)}) async-start(), calls=%async_computation.3 | async-start | bytes 4325376 | tf_op jit(solution)/shard_map/reduce_scatter | solution.py:97
  9.5 40.1 %copy-start.3 = (s32[32]{0:T(128)S(1)}, s32[32]{0:T(128)}, u32[]{:S(2)}) copy-start(s32[32]{0:T(128)} %param.17) | copy-start | bytes 388
Sparse Core Ops, SparseCore 0:
  9.8 39.7 all-gather.2
  51.4 35.9 all-gather.4
  184.5 151.4 reduce-scatter.1
where the time goes:
time: 345 us; the launch traced here: 344 us
  waiting for transfers between devices  188 us (54%)
  local copies, waits for them, and re-layouts  61.8 us (18%)
  matrix products  55.9 us (16%)
  other arithmetic  17.8 us (5%)
  between operations  13.9 us (4%)
  loops' own time  6.6 us (2%)
    reduce_scatter x1, waiting for transfers between devices, local(): lax.psum_scatter(partial_grads, ('ctx', 'head'), scatter_dimension=0, til...  150 us
    gather x16, local copies, waits for them, and re-layouts, visible(): key_doc = jnp.take(doc_tok, key_pos)  50.2 us
    all_gather x1, waiting for transfers between devices, local(): lax.all_gather(keys, 'ctx', axis=0, tiled=True)  36 us
    dot_general x16, matrix products, scores(): jnp.einsum('bhd,kd->bhk', queries, key_tile, preferred_element_type=jnp.f...  25.1 us
    dot_general x8, matrix products, grad_step(): jnp.einsum('bhk,kd->bhd', score_grad, key_tile, preferred_element_type=jn...  12.8 us
    dot_general x8, matrix products, grad_step(): jnp.einsum('bhd,kd->bhk', output_grad, value_tile, preferred_element_type...  10.8 us
  transfers between devices with their start and end apart: 3, of which 2 were waited for; matrix products, arithmetic and copies ran while one was open for 15% of the time, Pallas kernels for 0%

commit v1 on v0

--- a/solution.py
+++ b/solution.py
@@ -5,6 +5,11 @@
 
 BLK = 128
 masked_score = -1e30
+
+
+def gather_over(array, name, dim):
+    sent = jnp.stack([array] * lax.axis_size(name))
+    return jnp.concatenate(lax.all_to_all(sent, name, 0, 0), axis=dim)
 
 
 def local(queries, keys, values, output, output_grad, block_doc):
@@ -73,7 +78,7 @@
     )
     query_start = jnp.zeros((shard_rows, heads_here, head_size), jnp.float32)
     key_all, value_all = (
-        lax.all_gather(keys, "ctx", axis=0, tiled=True),
+        gather_over(keys, "ctx", 0),
         lax.all_gather(values, "ctx", axis=0, tiled=True),
     )
 

time: 345 us -> 322 us (0.933)
  matrix products: 55.9 us -> 33.9 us
  waiting for transfers between devices: 188 us -> 179 us
  starting transfers between devices: 0.11 us -> 6.11 us
    all_gather x1 -> x0, waiting for transfers between devices: 36 us -> none  [local(): lax.all_gather(keys, 'ctx', axis=0, tiled=True)]
    all_to_all x0 -> x1, waiting for transfers between devices: none -> 27 us  [gather_over(): return jnp.concatenate(lax.all_to_all(sent, name, 0, 0), axis=dim)]
    dot_general x16, matrix products: 25.1 us -> 10.7 us  [scores(): jnp.einsum('bhd,kd->bhk', queries, key_tile, preferred_element_type=jnp.f...]
    dot_general x8, matrix products: 12.8 us -> 5.45 us  [grad_step(): jnp.einsum('bhk,kd->bhd', score_grad, key_tile, preferred_element_type=jn...]
    all_to_all x0 -> x1, starting transfers between devices: none -> 6.03 us  [gather_over(): return jnp.concatenate(lax.all_to_all(sent, name, 0, 0), axis=dim)]
  transfers between devices with their start and end apart: 3 -> 3, of which waited for: 2 -> 2; matrix products, arithmetic and copies ran while one was open for 15% -> 13% of each run, Pallas kernels for 0% -> 0%
where the time goes in v1:
time: 322 us; the launch traced here: 321 us
  waiting for transfers between devices  179 us (56%)
  local copies, waits for them, and re-layouts  63.2 us (20%)
  matrix products  33.9 us (11%)
  other arithmetic  17.8 us (6%)
  between operations  14.2 us (4%)
  loops' own time  6.59 us (2%)
  starting transfers between devices  6.11 us (2%)
    reduce_scatter x1, waiting for transfers between devices, local(): lax.psum_scatter(partial_grads, ('ctx', 'head'), scatter_dimension=0, til...  152 us
    gather x16, local copies, waits for them, and re-layouts, visible(): key_doc = jnp.take(doc_tok, key_pos)  50.2 us
    all_to_all x1, waiting for transfers between devices, gather_over(): return jnp.concatenate(lax.all_to_all(sent, name, 0, 0), axis=dim)  27 us
    dot_general x8, matrix products, grad_step(): jnp.einsum('bhd,kd->bhk', output_grad, value_tile, preferred_element_type...  10.8 us
    dot_general x16, matrix products, scores(): jnp.einsum('bhd,kd->bhk', queries, key_tile, preferred_element_type=jnp.f...  10.7 us
    dynamic_update_slice x8, other arithmetic, local(): lax.scan(grad_loop, query_start, jnp.arange(cycle_length, dtype=jnp.int32))  6.73 us
  transfers between devices with their start and end apart: 3, of which 2 were waited for; matrix products, arithmetic and copies ran while one was open for 13% of the time, Pallas kernels for 0%

profile of v1, /device:TPU:24, one launch (start us, length us, event | category | flops | bytes accessed | tf_op | source)
XLA Modules:
  0.0 321.2 jit_solution(989101603923442751)
XLA Ops:
  7.2 2.1 stack.8
  9.3 6.0 %all-to-all-start = ((bf16[8,512,128]{2,1,0:T(8,128)(2,1)}), bf16[8,512,128]{2,1,0:T(8,128)(2,1)S(1)}, u32[]{:S(2)}, u32[]{:S(2)}) async-start(bf16[8,512,128]{2,1,0:T(8,128)(2,1)} %stack.8), calls=%async_computation | async-start | bytes 2097152 | tf_op jit(solution)/shard_map/all_to_all | solution.py:12
  15.4 0.7 all-gather.2.cloned.1.call-update
  16.3 0.6 multiply_reduce_fusion
  17.2 3.1 gather_fusion.2
  20.3 27.0 %all-to-all-done = bf16[8,512,128]{2,1,0:T(8,128)(2,1)S(1)} async-done(((bf16[8,512,128]{2,1,0:T(8,128)(2,1)}), bf16[8,512,128]{2,1,0:T(8,128)(2,1)S(1)}, u32[]{:S(2)}, u32[]{:S(2)}) %all-to-all-start) | async-done | bytes 1048608 | tf_op jit(solution)/shard_map/all_to_all | solution.py:12
  47.3 37.9 %while.29 = (s32[]{:T(128)}, f32[512,2]{0,1:T(2,128)S(1)}, f32[512,2]{0,1:T(2,128)S(1)}, s32[512]{0:T(512)S(1)}, bf16[4096,128]{1,0:T(8,128)(2,1)S(1)}, /*index=...) while((s32[]{:T(128)}, f32[512,2]{0,1:T(2,128)S(1)}, ...), condition=%wide.region_3.5_spmd.clone, body=%wide.region_0.4_spmd.clone.sunk | while | flops 139211264 | bytes 5474630 | solution.py:89
  47.4 3.1 gather_fusion
  52.2 3.1 gather_fusion
  56.9 3.1 gather_fusion
  61.6 3.1 gather_fusion
  66.4 3.1 gather_fusion
  71.1 3.1 gather_fusion
  75.9 3.1 gather_fusion
  80.6 3.1 gather_fusion
  85.3 74.8 %while.30 = (s32[]{:T(128)}, f32[512,2,128]{2,0,1:T(8,128)S(1)}, f32[8,512,2,128]{3,1,0,2:T(8,128)}, s32[8]{0:T(128)S(1)}, s32[512]{0:T(512)S(1)}, /*index=5*/bf...) while((s32[]{:T(128)}, f32[512,2,128]{2,0,1:T(8,128)S(1)}, ...), condition=%wide.region_6.8_spmd.clone, body=%wide.region_5.7_spmd.clone.sunk | while | flops 676666880 | bytes 14080389 | solution.py:98
  85.3 0.6 dynamic_slice.48
  86.6 3.1 gather_fusion.1
  90.1 0.8 fusion.77
  91.3 1.3 fusion.78
  93.1 0.7 fusion.79
  93.8 0.8 fusion.81
  94.7 0.6 dynamic_slice.48
  96.0 3.1 gather_fusion.1
  99.4 0.8 fusion.77
  100.7 1.3 fusion.78
  102.5 0.7 fusion.79
  103.2 0.8 fusion.81
  105.3 3.1 gather_fusion.1
  108.8 0.8 fusion.77
  110.0 1.3 fusion.78
  111.8 0.7 fusion.79
  112.5 0.9 fusion.81
  113.4 0.6 dynamic_slice.48
  114.7 3.1 gather_fusion.1
  118.1 0.8 fusion.77
  119.4 1.3 fusion.78
  121.2 0.7 fusion.79
  121.9 0.9 fusion.81
  124.1 3.1 gather_fusion.1
  127.5 0.8 fusion.77
  128.7 1.3 fusion.78
  130.5 0.7 fusion.79
  131.2 0.8 fusion.81
  133.4 3.1 gather_fusion.1
  136.9 0.8 fusion.77
  138.1 1.3 fusion.78
  139.9 0.7 fusion.79
  140.6 0.8 fusion.81
  142.8 3.1 gather_fusion.1
  146.2 0.8 fusion.77
  147.4 1.3 fusion.78
  149.2 0.7 fusion.79
  149.9 0.9 fusion.81
  150.8 0.6 dynamic_slice.48
  152.1 3.1 gather_fusion.1
  155.6 0.8 fusion.77
  156.8 1.3 fusion.78
  158.6 0.7 fusion.79
  159.3 0.8 fusion.81
  160.1 1.1 copy.33
  161.2 151.6 %reduce-scatter.2.cloned.1.call-done = f32[128,2,128]{2,0,1:T(8,128)} async-done(((f32[4096,2,128]{2,0,1:T(8,128)}), f32[128,2,128]{2,0,1:T(8,128)}) %reduce-scatter.2.cloned.1.call-update) | async-done | bytes 131088 | tf_op jit(solution)/shard_map/reduce_scatter | solution.py:102
  312.8 0.9 convert.4
  313.8 0.6 slice_bitcast_fusion
  (181 shorter events, 24.9 us)
Async XLA Ops:
  7.2 9.0 %copy-start.2 = (bf16[512,2,128]{2,1,0:T(2,128)(2,1)S(1)}, bf16[512,2,128]{2,1,0:T(2,128)(2,1)}, u32[]{:S(2)}) copy-start(bf16[512,2,128]{2,1,0:T(2,128)(2,1)} %param.12) | copy-start | bytes 786436
  7.2 9.0 %copy-start = (bf16[512,2,128]{2,1,0:T(2,128)(2,1)S(1)}, bf16[512,2,128]{2,1,0:T(2,128)(2,1)}, u32[]{:S(2)}) copy-start(bf16[512,2,128]{2,1,0:T(2,128)(2,1)} %param.16) | copy-start | bytes 786436
  7.2 9.1 %copy-start.1 = (bf16[512,2,128]{2,1,0:T(2,128)(2,1)S(1)}, bf16[512,2,128]{2,1,0:T(2,128)(2,1)}, u32[]{:S(2)}) copy-start(bf16[512,2,128]{2,1,0:T(2,128)(2,1)} %param.15) | copy-start | bytes 786436
  9.3 7.8 %copy-start.3 = (s32[32]{0:T(128)S(1)}, s32[32]{0:T(128)}, u32[]{:S(2)}) copy-start(s32[32]{0:T(128)} %param.17) | copy-start | bytes 388
  9.3 38.0 %all-to-all-start = ((bf16[8,512,128]{2,1,0:T(8,128)(2,1)}), bf16[8,512,128]{2,1,0:T(8,128)(2,1)S(1)}, u32[]{:S(2)}, u32[]{:S(2)}) async-start(bf16[8,512,128]{2,1,0:T(8,128)(2,1)} %stack.8), calls=%async_computation | async-start | bytes 2097152 | tf_op jit(solution)/shard_map/all_to_all | solution.py:12
  15.3 69.9 %all-gather.2.cloned.1.call-start = ((), (), s32[]{:S(2)}) async-start(), calls=%async_computation.2 | async-start | bytes 1179648 | tf_op jit(solution)/shard_map/all_gather | solution.py:82
  16.1 296.8 %reduce-scatter.2.cloned.1.call-start = ((), (), s32[]{:S(2)}) async-start(), calls=%async_computation.3 | async-start | bytes 4325376 | tf_op jit(solution)/shard_map/reduce_scatter | solution.py:102
Sparse Core Ops, SparseCore 0:
  17.9 38.6 all-gather.1
  160.2 152.5 reduce-scatter.1
